TPU v7x, 512 devices: a whole 4x4x16 slice. The times are simulated.
512 devices in a mesh: dp: 128 (over z, y, core), shard: 4 (over x).
Axes of the slice: x: 4, y: 4, z: 16, core: 2. Of those that a mesh axis runs over, the one named last changes fastest.
Arguments:
- key_grad: bfloat16 [128, 512, 2560], P('dp', 'shard'), may hold values from -90 to 90
- key_error: float32 [128, 512, 2560], P('dp', 'shard'), may hold values from -4 to 4
- router_grad: bfloat16 [128, 64, 2560], P('dp', 'shard'), may hold values from -90 to 90
- router_error: float32 [128, 64, 2560], P('dp', 'shard'), may hold values from -4 to 4
- norm_grad: bfloat16 [128, 2, 2560], P('dp', None, 'shard'), may hold values from -8 to 8
- key_basis: float32 [32, 2560], replicated, may hold values from -6 to 6
- router_basis: float32 [32, 2560], replicated, may hold values from -6 to 6
- key_momentum: float32 [512, 2560], P('shard', 'dp'), may hold values from -4 to 4
- key_weight: float32 [512, 2560], P('shard', 'dp'), may hold values from -4 to 4
- router_momentum: float32 [64, 2560], P('shard', 'dp'), may hold values from -4 to 4
- router_weight: float32 [64, 2560], P('shard', 'dp'), may hold values from -4 to 4
- norm_momentum: float32 [2, 2560], P(None, 'shard'), may hold values from -4 to 4
- norm_weight: float32 [2, 2560], P(None, 'shard'), may hold values from 0.5 to 1.5
Outputs:
- key_carry: float32 [128, 512, 2560], P('dp', 'shard')
- router_carry: float32 [128, 64, 2560], P('dp', 'shard')
- key_velocity: float32 [512, 2560], P('shard', 'dp')
- key_master: float32 [512, 2560], P('shard', 'dp')
- key_params: bfloat16 [512, 2560], P(None, 'dp')
- router_velocity: float32 [64, 2560], P('shard', 'dp')
- router_master: float32 [64, 2560], P('shard', 'dp')
- router_params: bfloat16 [64, 2560], P(None, 'dp')
- norm_velocity: float32 [2, 2560], P(None, 'shard')
- norm_master: float32 [2, 2560], P(None, 'shard')
- norm_params: bfloat16 [2, 2560], replicated
All inputs are finite; a program needn't handle non-finite values.
Results may differ from a plain program's by a relative error of at most 0.008.
Values may be sent and summed in bfloat16 or wider, within the bound.
No kernel may reach another device: no remote copies, remote signals or barrier semaphores. Data moves between devices by JAX's collectives and lax.ppermute only.
A program may use at most 64 MiB of HBM per device.

v0:
```python
import jax
import jax.numpy as jnp
from jax import lax
from jax.sharding import PartitionSpec as P

ROOT_STEPS = 4
highest = lax.Precision.HIGHEST
momentum_decay = 0.9
learning_rate = 0.1


def inverse_root(gram_matrix):
    scaling = jnp.sqrt(jnp.sum(gram_matrix * gram_matrix)) + 1e-06
    identity = jnp.eye(gram_matrix.shape[0], dtype=jnp.float32)
    square_side = gram_matrix / scaling
    root_side = identity
    for sweep_index in range(ROOT_STEPS):
        middle = 1.5 * identity - 0.5 * jnp.dot(root_side, square_side, precision=highest)
        square_side = jnp.dot(square_side, middle, precision=highest)
        root_side = jnp.dot(middle, root_side, precision=highest)
    return (root_side, scaling)


def project(old_basis, merged):
    return lax.dot_general(old_basis, merged, (((1,), (1,)), ((), ())), precision=highest)


def gram_of(factor_rows):
    return lax.dot_general(factor_rows, factor_rows, (((1,), (1,)), ((), ())), precision=highest)


def normalize(gram_matrix, factor_rows):
    root_side, scaling = inverse_root(gram_matrix)
    return jnp.dot(root_side, factor_rows, precision=highest) / jnp.sqrt(scaling)


def advance(momentum, weight, direction):
    velocity = momentum_decay * momentum + direction
    return (velocity, weight - learning_rate * velocity)


def body(
    key_grad,
    key_error,
    router_grad,
    router_error,
    norm_grad,
    key_basis,
    router_basis,
    key_momentum,
    key_weight,
    router_momentum,
    router_weight,
    norm_momentum,
    norm_weight,
):
    replicas = lax.axis_size("dp")
    rank_size = key_basis.shape[0]
    merged_key = key_grad[0].astype(jnp.float32) + key_error[0]
    merged_router = router_grad[0].astype(jnp.float32) + router_error[0]
    rows_key, rows_router, norm_sum = lax.psum(
        (
            project(key_basis, merged_key),
            project(router_basis, merged_router),
            norm_grad[0].astype(jnp.float32),
        ),
        "dp",
    )
    gram_key, gram_router = lax.psum((gram_of(rows_key), gram_of(rows_router)), "shard")
    ortho_key = normalize(gram_key, rows_key)
    ortho_router = normalize(gram_router, rows_router)
    key_part = lax.dot_general(merged_key, ortho_key, (((0,), (1,)), ((), ())), precision=highest)
    router_part = lax.dot_general(
        merged_router, ortho_router, (((0,), (1,)), ((), ())), precision=highest
    )
    column_sum = lax.psum(jnp.concatenate([key_part, router_part], axis=1), ("dp", "shard"))
    columns = column_sum / replicas
    approx_key = lax.dot_general(
        ortho_key, columns[:, :rank_size], (((0,), (1,)), ((), ())), precision=highest
    )
    approx_router = lax.dot_general(
        ortho_router, columns[:, rank_size:], (((0,), (1,)), ((), ())), precision=highest
    )
    col_width = key_momentum.shape[1]
    offset = lax.axis_index("dp") * col_width
    key_velocity, key_master = advance(
        key_momentum, key_weight, lax.dynamic_slice_in_dim(approx_key, offset, col_width, 1)
    )
    router_velocity, router_master = advance(
        router_momentum,
        router_weight,
        lax.dynamic_slice_in_dim(approx_router, offset, col_width, 1),
    )
    norm_velocity, norm_master = advance(norm_momentum, norm_weight, norm_sum / replicas)
    key_params, router_params, norm_params = (
        lax.all_gather(key_master.astype(jnp.bfloat16), "shard", axis=0, tiled=True),
        lax.all_gather(router_master.astype(jnp.bfloat16), "shard", axis=0, tiled=True),
        lax.all_gather(norm_master.astype(jnp.bfloat16), "shard", axis=1, tiled=True),
    )
    key_carry = (merged_key - approx_key)[None]
    router_carry = (merged_router - approx_router)[None]
    return (
        key_carry,
        router_carry,
        key_velocity,
        key_master,
        key_params,
        router_velocity,
        router_master,
        router_params,
        norm_velocity,
        norm_master,
        norm_params,
    )


def solution(mesh):
    return jax.shard_map(
        body,
        mesh=mesh,
        in_specs=(
            P("dp", "shard", None),
            P("dp", "shard", None),
            P("dp", "shard", None),
            P("dp", "shard", None),
            P("dp", None, "shard"),
            P(),
            P(),
            P("shard", "dp"),
            P("shard", "dp"),
            P("shard", "dp"),
            P("shard", "dp"),
            P(None, "shard"),
            P(None, "shard"),
        ),
        out_specs=(
            P("dp", "shard", None),
            P("dp", "shard", None),
            P("shard", "dp"),
            P("shard", "dp"),
            P(None, "dp"),
            P("shard", "dp"),
            P("shard", "dp"),
            P(None, "dp"),
            P(None, "shard"),
            P(None, "shard"),
            P(),
        ),
        check_vma=False,
    )
```

profile of v0, /device:TPU:8, one launch (start us, length us, event | category | flops | bytes accessed | tf_op | source)
XLA Modules:
  0.0 1036.4 jit_solution(1657459035492836335)
XLA Ops:
  7.2 0.0 copy-start
  7.2 0.0 all-reduce.4.cloned.1.call-start
  7.2 0.7 bitcast_convert_fusion
  8.0 1.4 convolution_bitcast_fusion
  9.4 0.0 copy-done
  9.5 0.0 copy-start.2
  9.5 2.9 fusion.5
  12.4 497.1 %all-reduce = (f32[32,128]{1,0:T(8,128)S(1)}, f32[32,16]{0,1:T(8,128)S(1)}, f32[2,640]{1,0:T(2,128)S(1)}) all-reduce(f32[32,128]{1,0:T(8,128)S(1)} %fusion.5, f32[32,16]{0,1:T(8,128)S(1)} %convolution_bitcast_fusion, f32[2,640]{1,0:T(2,128)S(1)} %bitcast_convert_fusion), channel_id=1, replica_groups=mesh['dp'=128,'shard'=4] {'dp'}, use_global_device_ids=true, to_apply=%region_0.0 | all-reduce | flops 5888 | bytes 47104 | tf_op jit(solution)/shard_map/psum | solution.py:61
  509.5 0.1 fusion.31
  509.6 0.2 fusion.37
  509.9 17.1 %all-reduce.1 = (f32[32,32]{1,0:T(8,128)S(1)}, f32[32,32]{1,0:T(8,128)S(1)}) all-reduce(f32[32,32]{1,0:T(8,128)S(1)} %fusion.31, f32[32,32]{1,0:T(8,128)S(1)} %fusion.37), channel_id=1, replica_groups=mesh['dp'=128,'shard'=4] {'shard'}, use_global_device_ids=true, to_apply=%region_1.0 | all-reduce | flops 2048 | bytes 16384 | tf_op jit(solution)/shard_map/psum | solution.py:69
  527.0 0.6 multiply_reduce_fusion
  528.3 0.1 fusion.11
  528.4 0.1 fusion.27
  528.6 0.1 fusion.24
  528.7 0.2 fusion.10
  528.9 0.1 fusion.39
  529.0 0.1 fusion.38
  529.2 0.2 fusion.9
  529.3 0.1 fusion.40
  529.5 0.1 fusion.41
  530.4 0.1 fusion.15
  530.5 0.1 fusion.26
  530.7 0.1 fusion.25
  530.8 0.2 fusion.14
  531.0 0.1 fusion.33
  531.1 0.1 fusion.32
  531.3 0.2 fusion.13
  531.4 0.1 fusion.34
  531.6 0.0 copy-start.3
  531.6 0.0 copy-start.4
  531.6 0.1 fusion.35
  531.7 0.2 fusion.8
  531.9 0.1 fusion.42
  532.0 0.2 fusion.12
  532.2 0.1 fusion.36
  532.3 0.2 convolution_divide_fusion
  532.5 0.9 fusion
  533.5 0.1 convolution_divide_fusion.1
  533.6 0.0 copy-done.3
  533.6 0.0 copy-start.5
  533.6 0.5 fusion.20
  534.1 0.9 pad_maximum_fusion
  535.0 0.0 all-reduce.4.cloned.1.call-update
  535.0 0.6 fusion.28
  535.6 11.8 %all_gather.11 = bf16[2,2560]{1,0:T(2,128)(2,1)S(1)} all-gather(bf16[2,640]{1,0:T(2,128)(2,1)S(1)} %get-tuple-element.27), channel_id=1, replica_groups=mesh['dp'=128,'shard'=4] {'shard'}, dimensions={1}, use_global_device_ids=true | all-gather | bytes 12800 | tf_op jit(solution)/shard_map/all_gather | solution.py:98
  547.4 0.1 copy.24
  547.5 0.1 copy.25
  547.6 445.8 %all-reduce.4.cloned.1.call-done = f32[2560,64]{0,1:T(8,128)} async-done(((f32[2560,64]{0,1:T(8,128)}), f32[2560,64]{0,1:T(8,128)}) %all-reduce.4.cloned.1.call-update) | async-done | bytes 655376 | tf_op jit(solution)/shard_map/psum | solution.py:76
  993.4 1.1 broadcast_multiply_fusion
  994.6 0.0 copy-start.7
  994.6 0.3 fusion.16
  994.9 2.3 fusion.18
  997.2 0.7 fusion.23
  997.9 0.7 fusion.29
  998.6 12.0 %all_gather.10 = bf16[64,20]{1,0:T(8,128)(2,1)S(1)} all-gather(bf16[16,20]{1,0:T(8,128)(2,1)S(1)} %get-tuple-element.30), channel_id=1, replica_groups=mesh['dp'=128,'shard'=4] {'shard'}, dimensions={0}, use_global_device_ids=true | all-gather | bytes 3200 | tf_op jit(solution)/shard_map/all_gather | solution.py:97
  1010.6 0.7 copy.29
  1011.3 2.6 fusion.4
  1013.9 1.0 fusion.30
  1014.8 0.7 copy.27
  1015.5 0.7 copy.26
  1016.2 12.0 %all_gather.9 = bf16[512,20]{1,0:T(8,128)(2,1)S(1)} all-gather(bf16[128,20]{1,0:T(8,128)(2,1)S(1)} %get-tuple-element.33), channel_id=1, replica_groups=mesh['dp'=128,'shard'=4] {'shard'}, dimensions={0}, use_global_device_ids=true | all-gather | bytes 25600 | tf_op jit(solution)/shard_map/all_gather | solution.py:96
  1028.2 0.7 copy.28
  1028.9 0.6 copy.32
  (14 shorter events, 0.0 us)
Async XLA Ops:
  7.2 2.3 copy-start
  7.2 986.2 %all-reduce.4.cloned.1.call-start = ((), (), s32[]{:S(2)}) async-start(), calls=%async_computation | async-start | bytes 1310720 | tf_op jit(solution)/shard_map/psum | solution.py:76
  9.4 523.1 %copy-start.1 = (f32[1,128,2560]{2,1,0:T(8,128)S(1)}, f32[1,128,2560]{2,1,0:T(8,128)}, u32[]{:S(2)}) copy-start(f32[1,128,2560]{2,1,0:T(8,128)} %param.14) | copy-start | bytes 3932164
  9.5 523.1 %copy-start.2 = (bf16[1,128,2560]{2,1,0:T(8,128)(2,1)S(1)}, bf16[1,128,2560]{2,1,0:T(8,128)(2,1)}, u32[]{:S(2)}) copy-start(bf16[1,128,2560]{2,1,0:T(8,128)(2,1)} %param.13) | copy-start | bytes 1966084
  531.6 2.0 copy-start.3
  531.6 2.0 copy-start.4
  533.4 1.6 copy-start.9
  533.4 1.6 copy-start.10
  533.6 13.8 %copy-start.5 = (f32[128,20]{0,1:T(8,128)S(1)}, f32[128,20]{0,1:T(8,128)}, u32[]{:S(2)}) copy-start(f32[128,20]{0,1:T(8,128)} %param.20) | copy-start | bytes 30724
  533.6 13.9 %copy-start.6 = (f32[128,20]{0,1:T(8,128)S(1)}, f32[128,20]{0,1:T(8,128)}, u32[]{:S(2)}) copy-start(f32[128,20]{0,1:T(8,128)} %param.21) | copy-start | bytes 30724
  994.6 3.3 copy-start.7
  994.6 3.3 copy-start.8
Sparse Core Ops, SparseCore 0:
  535.1 458.2 all-reduce.3
where the time goes:
time: 1040 us
  blocking collectives  550 us (53%)
  waiting for transfers between devices  446 us (43%)
  between operations  15.8 us (2%)
  matrix products  12.1 us (1%)
    psum x1, blocking collectives, body(): lax.psum((project(key_basis, merged_key), project(router_basis, merged_ro...  497 us
    psum x1, waiting for transfers between devices, body(): lax.psum(jnp.concatenate([key_part, router_part], axis=1), ('dp', 'shard'))  446 us
  transfers between devices with their start and end apart: 1, of which 1 were waited for; matrix products, arithmetic and copies ran while one was open for 0% of the time, Pallas kernels for 0%

commit v1 on v0

--- a/solution.py
+++ b/solution.py
@@ -73,7 +73,8 @@
     router_part = lax.dot_general(
         merged_router, ortho_router, (((0,), (1,)), ((), ())), precision=highest
     )
-    column_sum = lax.psum(jnp.concatenate([key_part, router_part], axis=1), ("dp", "shard"))
+    one_axis = lax.psum(jnp.concatenate([key_part, router_part], axis=1), "shard")
+    column_sum = lax.psum(one_axis, "dp")
     columns = column_sum / replicas
     approx_key = lax.dot_general(
         ortho_key, columns[:, :rank_size], (((0,), (1,)), ((), ())), precision=highest

time: 1040 us -> 975 us (0.938)
  the two profiles are of different devices: /device:TPU:8 before, /device:TPU:2 now
where the time goes in v1:
time: 975 us
  blocking collectives  552 us (57%)
  waiting for transfers between devices  382 us (39%)
  between operations  15.9 us (2%)
  matrix products  12.1 us (1%)
    psum x1, blocking collectives, body(): lax.psum((project(key_basis, merged_key), project(router_basis, merged_ro...  502 us
    psum x1, waiting for transfers between devices, body(): column_sum = lax.psum(one_axis, 'dp')  330 us
    psum x1, waiting for transfers between devices, body(): lax.psum(jnp.concatenate([key_part, router_part], axis=1), 'shard')  52.4 us
  transfers between devices with their start and end apart: 2, of which 2 were waited for; matrix products, arithmetic and copies ran while one was open for 0% of the time, Pallas kernels for 0%

profile of v1, /device:TPU:2, one launch (start us, length us, event | category | flops | bytes accessed | tf_op | source)
XLA Modules:
  0.0 974.6 jit_solution(10453473724287904602)
XLA Ops:
  7.2 0.0 copy-start
  7.2 0.0 all-reduce.5.cloned.1.call-start
  7.2 0.7 bitcast_convert_fusion
  8.0 1.4 convolution_bitcast_fusion
  9.4 0.0 copy-done
  9.5 0.0 copy-start.2
  9.5 2.9 fusion.5
  12.4 502.2 %all-reduce = (f32[32,128]{1,0:T(8,128)S(1)}, f32[32,16]{0,1:T(8,128)S(1)}, f32[2,640]{1,0:T(2,128)S(1)}) all-reduce(f32[32,128]{1,0:T(8,128)S(1)} %fusion.5, f32[32,16]{0,1:T(8,128)S(1)} %convolution_bitcast_fusion, f32[2,640]{1,0:T(2,128)S(1)} %bitcast_convert_fusion), channel_id=1, replica_groups=mesh['dp'=128,'shard'=4] {'dp'}, use_global_device_ids=true, to_apply=%region_0.0 | all-reduce | flops 5888 | bytes 47104 | tf_op jit(solution)/shard_map/psum | solution.py:61
  514.6 0.1 fusion.31
  514.8 0.2 fusion.37
  515.0 14.1 %all-reduce.1 = (f32[32,32]{1,0:T(8,128)S(1)}, f32[32,32]{1,0:T(8,128)S(1)}) all-reduce(f32[32,32]{1,0:T(8,128)S(1)} %fusion.31, f32[32,32]{1,0:T(8,128)S(1)} %fusion.37), channel_id=1, replica_groups=mesh['dp'=128,'shard'=4] {'shard'}, use_global_device_ids=true, to_apply=%region_1.0 | all-reduce | flops 2048 | bytes 16384 | tf_op jit(solution)/shard_map/psum | solution.py:69
  529.1 0.6 multiply_reduce_fusion
  530.5 0.1 fusion.11
  530.6 0.1 fusion.27
  530.8 0.1 fusion.24
  530.9 0.2 fusion.10
  531.1 0.1 fusion.39
  531.2 0.1 fusion.38
  531.4 0.2 fusion.9
  531.5 0.1 fusion.40
  531.7 0.1 fusion.41
  532.6 0.1 fusion.15
  532.7 0.1 fusion.26
  532.9 0.1 fusion.25
  533.0 0.2 fusion.14
  533.2 0.1 fusion.33
  533.3 0.1 fusion.32
  533.4 0.2 fusion.13
  533.6 0.1 fusion.34
  533.8 0.0 copy-start.3
  533.8 0.1 fusion.35
  533.9 0.2 fusion.8
  534.1 0.1 fusion.42
  534.2 0.2 fusion.12
  534.4 0.1 fusion.36
  534.5 0.2 convolution_divide_fusion
  534.7 0.9 fusion
  535.6 0.1 convolution_divide_fusion.1
  535.7 0.0 copy-done.3
  535.8 0.5 fusion.20
  536.3 0.9 pad_maximum_fusion
  537.2 0.0 all-reduce.5.cloned.1.call-update
  537.2 0.0 all-reduce.7.cloned.1.call-start
  537.2 52.4 %all-reduce.5.cloned.1.call-done = f32[2560,64]{0,1:T(8,128)} async-done(((f32[2560,64]{0,1:T(8,128)}), f32[2560,64]{0,1:T(8,128)}) %all-reduce.5.cloned.1.call-update) | async-done | bytes 655376 | tf_op jit(solution)/shard_map/psum | solution.py:76
  589.7 0.0 all-reduce.7.cloned.1.call-update
  589.7 0.6 fusion.28
  590.3 11.5 %all_gather.11 = bf16[2,2560]{1,0:T(2,128)(2,1)S(1)} all-gather(bf16[2,640]{1,0:T(2,128)(2,1)S(1)} %get-tuple-element.27), channel_id=1, replica_groups=mesh['dp'=128,'shard'=4] {'shard'}, dimensions={1}, use_global_device_ids=true | all-gather | bytes 12800 | tf_op jit(solution)/shard_map/all_gather | solution.py:99
  601.8 0.1 copy.24
  601.9 0.1 copy.25
  602.0 329.7 %all-reduce.7.cloned.1.call-done = f32[2560,64]{0,1:T(8,128)} async-done(((f32[2560,64]{0,1:T(8,128)}), f32[2560,64]{0,1:T(8,128)}) %all-reduce.7.cloned.1.call-update) | async-done | bytes 655376 | tf_op jit(solution)/shard_map/psum | solution.py:77
  931.7 1.1 broadcast_multiply_fusion
  932.9 0.3 fusion.16
  933.2 2.3 fusion.18
  935.5 0.7 fusion.23
  936.2 0.7 fusion.29
  936.9 11.9 %all_gather.10 = bf16[64,20]{1,0:T(8,128)(2,1)S(1)} all-gather(bf16[16,20]{1,0:T(8,128)(2,1)S(1)} %get-tuple-element.30), channel_id=1, replica_groups=mesh['dp'=128,'shard'=4] {'shard'}, dimensions={0}, use_global_device_ids=true | all-gather | bytes 3200 | tf_op jit(solution)/shard_map/all_gather | solution.py:98
  948.8 0.7 copy.29
  949.5 2.6 fusion.4
  952.1 1.0 fusion.30
  953.1 0.7 copy.27
  953.7 0.7 copy.26
  954.4 12.0 %all_gather.9 = bf16[512,20]{1,0:T(8,128)(2,1)S(1)} all-gather(bf16[128,20]{1,0:T(8,128)(2,1)S(1)} %get-tuple-element.33), channel_id=1, replica_groups=mesh['dp'=128,'shard'=4] {'shard'}, dimensions={0}, use_global_device_ids=true | all-gather | bytes 25600 | tf_op jit(solution)/shard_map/all_gather | solution.py:97
  966.4 0.7 copy.28
  967.1 0.6 copy.33
  (17 shorter events, 0.1 us)
Async XLA Ops:
  7.2 2.3 copy-start
  7.2 582.5 %all-reduce.5.cloned.1.call-start = ((), (), s32[]{:S(2)}) async-start(), calls=%async_computation | async-start | bytes 1310720 | tf_op jit(solution)/shard_map/psum | solution.py:76
  9.4 525.2 %copy-start.1 = (f32[1,128,2560]{2,1,0:T(8,128)S(1)}, f32[1,128,2560]{2,1,0:T(8,128)}, u32[]{:S(2)}) copy-start(f32[1,128,2560]{2,1,0:T(8,128)} %param.14) | copy-start | bytes 3932164
  9.5 525.2 %copy-start.2 = (bf16[1,128,2560]{2,1,0:T(8,128)(2,1)S(1)}, bf16[1,128,2560]{2,1,0:T(8,128)(2,1)}, u32[]{:S(2)}) copy-start(bf16[1,128,2560]{2,1,0:T(8,128)(2,1)} %param.13) | copy-start | bytes 1966084
  533.8 2.0 copy-start.3
  533.8 2.0 copy-start.4
  536.2 53.5 %copy-start.9 = (f32[2,640]{1,0:T(2,128)S(1)}, f32[2,640]{1,0:T(2,128)}, u32[]{:S(2)}) copy-start(f32[2,640]{1,0:T(2,128)} %param.25) | copy-start | bytes 15364
  536.3 53.4 %copy-start.10 = (f32[2,640]{1,0:T(2,128)S(1)}, f32[2,640]{1,0:T(2,128)}, u32[]{:S(2)}) copy-start(f32[2,640]{1,0:T(2,128)} %param.24) | copy-start | bytes 15364
  536.3 65.5 %copy-start.5 = (f32[128,20]{0,1:T(8,128)S(1)}, f32[128,20]{0,1:T(8,128)}, u32[]{:S(2)}) copy-start(f32[128,20]{0,1:T(8,128)} %param.20) | copy-start | bytes 30724
  536.3 65.6 %copy-start.6 = (f32[128,20]{0,1:T(8,128)S(1)}, f32[128,20]{0,1:T(8,128)}, u32[]{:S(2)}) copy-start(f32[128,20]{0,1:T(8,128)} %param.21) | copy-start | bytes 30724
  537.2 394.6 %all-reduce.7.cloned.1.call-start = ((), (), s32[]{:S(2)}) async-start(), calls=%async_computation.1 | async-start | bytes 1310720 | tf_op jit(solution)/shard_map/psum | solution.py:77
  932.9 3.3 copy-start.7
  932.9 3.3 copy-start.8
Sparse Core Ops, SparseCore 0:
  537.3 52.2 all-reduce.4
  593.1 338.6 all-reduce.6
